TPU v7x, 512 devices: a whole 4x4x16 slice. The times are simulated.
512 devices in a mesh: aa: 32 (over z, core), ba: 16 (over x, y).
Axes of the slice: x: 4, y: 4, z: 16, core: 2. Of those that a mesh axis runs over, the one named last changes fastest.
Arguments:
- right_sides: bfloat16 [524288, 512], P(('aa', 'ba')), may hold values from -6 to 6
- point_order: int32 [512, 1024], P(('aa', 'ba')), may hold values from 0 to 1023, each once within a row
- skeleton: int32 [512, 128], P(('aa', 'ba')), may hold values from 0 to 1023, as said below
- leaf_inverse: bfloat16 [524288, 1024], P(('aa', 'ba')), may hold values from -1 to 3.5
- leaf_basis: bfloat16 [524288, 128], P(('aa', 'ba')), may hold values from -0.1875 to 0.1875
- group_core: bfloat16 [65536, 2048], P(('aa', 'ba')), may hold values from -1 to 2, as said below
- transfer: float32 [65536, 128], P(('aa', 'ba')), may hold values from -0.5 to 0.5
- top_core: bfloat16 [4096, 4096], P(('aa', 'ba')), may hold values from -1 to 2
Outputs:
- solution: bfloat16 [524288, 512], P(('aa', 'ba'))
Inputs may be any that keep to these rules, and one draw needn't show every extreme that they name: `skeleton`: each row holds 128 different indices in increasing order. `group_core`: each group's block of 2048 rows is symmetric.
All inputs are finite; a program needn't handle non-finite values.
Results may differ from a plain program's by a relative error of at most 0.014.
Values may be sent and summed in bfloat16 or wider, within the bound.
A program may use at most 64 MiB of HBM per device.

v0:
```python
import jax
import jax.numpy as jnp
from jax import lax
from jax.sharding import PartitionSpec as P


def from_everyone(value, axis):
    copies = jnp.broadcast_to(value, (lax.axis_size(axis), *value.shape))
    return lax.all_to_all(copies, axis, split_axis=0, concat_axis=0, tiled=True)


def in_order(parts, dim):
    parts = jnp.moveaxis(parts, 0, dim)
    dims = parts.shape
    return parts.reshape(*dims[:dim], dims[dim] * dims[dim + 1], *dims[dim + 2 :])


def gathered_copies(value, axis, dim):
    parts = from_everyone(value, axis)
    return in_order(parts, dim)


def taken_together(value, axis):
    everything = from_everyone(value, axis)
    return jnp.sum(everything.astype(jnp.float32), axis=0)


def shards(
    right_sides, point_order, skeleton, leaf_inverse, leaf_basis, group_core, transfer, top_core
):
    ordering = point_order[0]
    skel_rows = skeleton[0]
    rows_matrix = gathered_copies(top_core, "ba", 0)
    ordered = jnp.take(right_sides, ordering, axis=0)
    applied = jnp.dot(leaf_inverse, ordered, preferred_element_type=jnp.float32)
    applied_low = applied.astype(jnp.bfloat16)
    coeffs = jnp.einsum("lr,lc->rc", leaf_basis, applied_low, preferred_element_type=jnp.float32)
    coeffs = coeffs + jnp.take(applied, skel_rows, axis=0)
    coeff_low = coeffs.astype(jnp.bfloat16)
    level_one = jnp.dot(
        group_core, gathered_copies(coeff_low, "ba", 0), preferred_element_type=jnp.float32
    )
    remainder = coeffs - level_one
    partial_value = jnp.einsum("rs,rc->sc", transfer, remainder, precision=lax.Precision.HIGHEST)
    group_coeffs = taken_together(partial_value.astype(jnp.bfloat16), "ba").astype(jnp.float32)
    folded = jnp.dot(
        rows_matrix,
        lax.all_gather(group_coeffs.astype(jnp.bfloat16), "aa", axis=0, tiled=True),
        preferred_element_type=jnp.float32,
    )
    correction = level_one + jnp.einsum(
        "rs,sc->rc", transfer, folded, precision=lax.Precision.HIGHEST
    )
    expanded = jnp.dot(
        leaf_basis, correction.astype(jnp.bfloat16), preferred_element_type=jnp.float32
    )
    expanded = expanded.at[skel_rows].add(correction)
    solved = applied - jnp.dot(
        leaf_inverse, expanded.astype(jnp.bfloat16), preferred_element_type=jnp.float32
    )
    placed = jnp.zeros(solved.shape, jnp.bfloat16)
    return placed.at[ordering].set(solved.astype(jnp.bfloat16))


def solution(mesh):
    in_specs = (
        P(("aa", "ba"), None),
        P(("aa", "ba"), None),
        P(("aa", "ba"), None),
        P(("aa", "ba"), None),
        P(("aa", "ba"), None),
        P(("aa", "ba"), None),
        P(("aa", "ba"), None),
        P(("aa", "ba"), None),
    )
    out_specs = P(("aa", "ba"), None)
    return jax.shard_map(shards, mesh=mesh, in_specs=in_specs, out_specs=out_specs, check_vma=False)
```

profile of v0, /device:TPU:1, one launch (start us, length us, event | category | flops | bytes accessed | tf_op | source)
XLA Modules:
  0.0 204.4 jit_solution(15782101160970093761)
XLA Ops:
  6.5 0.8 fusion.15
  7.3 0.7 compare_and_fusion.1
  8.0 0.7 compare_select_fusion
  8.7 0.7 compare_and_fusion
  9.4 5.4 %gather_fusion = bf16[1024,512]{1,0:T(8,128)(2,1)S(1)} fusion(bf16[1024,512]{1,0:T(8,128)(2,1)} %param.8, s32[1024]{0:T(1024)S(1)} %broadcast_clamp_fusion), kind=kCustom, calls=%fused_computation | custom fusion | bytes 2101248 | tf_op jit(solution)/shard_map/jit(_take)/gather | solution.py:34
  14.8 2.9 %convolution_bitcast_fusion = f32[1024,512]{0,1:T(8,128)} fusion(bf16[1024,1024]{1,0:T(8,128)(2,1)S(1)} %copy-done, bf16[1024,512]{1,0:T(8,128)(2,1)S(1)} %gather_fusion, pred[1024]{0:T(1024)(128)(4,1)S(1)} %compare_and_fusion), kind=kOutput, calls=%fused_computation.6 | convolution fusion | flops 1074266112 | bytes 5243904 | tf_op jit(solution)/shard_map/dot_general | solution.py:35
  17.7 2.9 %copy.21 = f32[1024,512]{1,0:T(8,128)} copy(f32[1024,512]{0,1:T(8,128)} %convolution_bitcast_fusion) | data formatting | bytes 4194304 | tf_op jit(solution)/shard_map/dot_general | solution.py:35
  20.6 2.5 %gather_fusion.1 = f32[128,512]{1,0:T(8,128)S(1)} fusion(f32[1024,512]{1,0:T(8,128)} %copy.21, s32[1024]{0:T(1024)S(1)} %pad_clamp_fusion), kind=kCustom, calls=%fused_computation.1 | custom fusion | bytes 524800 | tf_op jit(solution)/shard_map/jit(_take)/gather | solution.py:38
  23.1 0.1 copy.22
  23.3 2.0 fusion.17
  25.3 0.1 copy.23
  25.4 0.2 broadcast_in_dim.39
  25.6 33.7 %all_to_all.15 = bf16[16,128,512]{2,1,0:T(8,128)(2,1)S(1)} all-to-all(bf16[16,128,512]{2,1,0:T(8,128)(2,1)S(1)} %broadcast_in_dim.39), channel_id=1, replica_groups=mesh['aa'=32,'ba'=16] {'ba'}, dimensions={0} | all-to-all | bytes 4194304 | tf_op jit(solution)/shard_map/all_to_all | solution.py:9
  59.4 0.7 convolution_bitcast_fusion.2
  60.1 0.1 copy-done.3
  60.2 0.4 fusion.3
  60.6 0.1 copy.24
  60.7 0.2 broadcast_in_dim.40
  60.9 28.3 %all_to_all.16 = bf16[16,128,512]{2,1,0:T(8,128)(2,1)} all-to-all(bf16[16,128,512]{2,1,0:T(8,128)(2,1)S(1)} %broadcast_in_dim.40), channel_id=1, replica_groups=mesh['aa'=32,'ba'=16] {'ba'}, dimensions={0} | all-to-all | bytes 4194304 | tf_op jit(solution)/shard_map/all_to_all | solution.py:9
  89.2 2.6 %reduce_sum.12 = bf16[128,512]{1,0:T(8,128)(2,1)} reduce(bf16[16,128,512]{2,1,0:T(8,128)(2,1)} %all_to_all.16, bf16[]{:T(256)} %constant.19.clone.1), dimensions={0}, to_apply=%region_0.1 | reduce | flops 983040 | bytes 2228226 | tf_op jit(solution)/shard_map/reduce_sum | solution.py:25
  91.8 0.1 broadcast_in_dim.41
  91.9 17.2 %all_to_all.17 = bf16[16,8,4096]{2,1,0:T(8,128)(2,1)S(1)} all-to-all(bf16[16,8,4096]{2,1,0:T(8,128)(2,1)S(1)} %broadcast_in_dim.41), channel_id=1, replica_groups=mesh['aa'=32,'ba'=16] {'ba'}, dimensions={0} | all-to-all | bytes 2097152 | tf_op jit(solution)/shard_map/all_to_all | solution.py:9
  109.1 62.5 %all-gather.2.cloned.1.call-done = bf16[4096,512]{1,0:T(8,128)(2,1)} async-done(((bf16[128,512]{1,0:T(8,128)(2,1)}), bf16[4096,512]{1,0:T(8,128)(2,1)}) %all-gather.2.cloned.1.call-update) | async-done | bytes 4194320 | tf_op jit(solution)/shard_map/all_gather | solution.py:48
  171.6 3.5 %fusion.4 = f32[512,128]{1,0:T(8,128)S(1)} fusion(bf16[4096,512]{1,0:T(8,128)(2,1)} %all-gather.2.cloned.1.call-done, bf16[16,8,4096]{2,1,0:T(8,128)(2,1)S(1)} %all_to_all.17), kind=kOutput, calls=%fused_computation.15 | convolution fusion | flops 536870912 | bytes 5505024 | tf_op jit(solution)/shard_map/dot_general | solution.py:46
  175.1 0.4 fusion.1
  175.5 0.1 copy.26
  175.6 2.7 %convolution_bitcast_fusion.1 = f32[1024,512]{0,1:T(8,128)} fusion(bf16[1024,128]{1,0:T(8,128)(2,1)} %param.12, f32[128,512]{0,1:T(8,128)S(1)} %fusion.1), kind=kOutput, calls=%fused_computation.7 | convolution fusion | flops 134283264 | bytes 2621440 | tf_op jit(solution)/shard_map/dot_general | solution.py:54
  178.3 2.9 %copy.25 = f32[1024,512]{1,0:T(8,128)} copy(f32[1024,512]{0,1:T(8,128)} %convolution_bitcast_fusion.1) | data formatting | bytes 4194304 | tf_op jit(solution)/shard_map/dot_general | solution.py:54
  181.3 4.2 %scatter_fusion = f32[1024,512]{1,0:T(8,128)} fusion(f32[1024,512]{1,0:T(8,128)} %copy.25, s32[128]{0:T(128)S(1)} %fusion.15, f32[128,512]{1,0:T(8,128)S(1)} %copy.26), kind=kCustom, calls=%fused_computation.2 | custom fusion | flops 65536 | bytes 786944 | tf_op jit(solution)/shard_map/scatter-add | solution.py:57
  185.5 4.5 %fusion = bf16[1024,512]{0,1:T(8,128)(2,1)} fusion(f32[1024,512]{0,1:T(8,128)} %convolution_bitcast_fusion, bf16[1024,1024]{1,0:T(8,128)(2,1)S(1)} %copy-done, f32[1024,512]{1,0:T(8,128)} %scatter_fusion), kind=kOutput, calls=%fused_computation.5 | convolution fusion | flops 1075314688 | bytes 7340032 | tf_op jit(solution)/shard_map/dot_general | solution.py:58
  190.0 1.5 copy.27
  191.5 6.1 %scatter_custom_fusion.1 = bf16[1024,512]{1,0:T(8,128)(2,1)} fusion(s32[1024]{0:T(1024)S(1)} %bitcast.48, bf16[1024,512]{1,0:T(8,128)(2,1)S(1)} %copy.27, bf16[]{:T(256)} %constant.19.clone.1), kind=kCustom, calls=%fused_computation.22 | custom fusion | bytes 1048578 | tf_op jit(solution)/shard_map/scatter | solution.py:62
  (13 shorter events, 0.0 us)
Async XLA Ops:
  6.5 8.2 %copy-start = (bf16[1024,1024]{1,0:T(8,128)(2,1)S(1)}, bf16[1024,1024]{1,0:T(8,128)(2,1)}, u32[]{:S(2)}) copy-start(bf16[1024,1024]{1,0:T(8,128)(2,1)} %param.11) | copy-start | bytes 6291460
  6.5 165.1 %all-gather.2.cloned.1.call-start = ((), (), s32[]{:S(2)}) async-start(), calls=%async_computation.3 | async-start | bytes 4325376 | tf_op jit(solution)/shard_map/all_gather | solution.py:48
  20.6 2.6 %copy-start.1 = (bf16[1024,128]{1,0:T(8,128)(2,1)S(1)}, bf16[1024,128]{1,0:T(8,128)(2,1)}, u32[]{:S(2)}) copy-start(bf16[1024,128]{1,0:T(8,128)(2,1)} %param.12) | copy-start | bytes 786436
  25.6 33.8 %copy-start.2 = (bf16[128,2048]{1,0:T(8,128)(2,1)S(1)}, bf16[128,2048]{1,0:T(8,128)(2,1)}, u32[]{:S(2)}) copy-start(bf16[128,2048]{1,0:T(8,128)(2,1)} %param.13) | copy-start | bytes 1572868
  59.4 0.8 copy-start.3
  89.2 2.6 %copy-start.4 = (bf16[8,4096]{1,0:T(8,128)(2,1)S(1)}, bf16[8,4096]{1,0:T(8,128)(2,1)}, u32[]{:S(2)}) copy-start(bf16[8,4096]{1,0:T(8,128)(2,1)} %param.15) | copy-start | bytes 196612
Sparse Core Ops, SparseCore 0:
  91.9 79.6 all-gather.1
where the time goes:
time: 205 us; the launch traced here: 204 us
  blocking collectives  79.2 us (39%)
  waiting for transfers between devices  62.5 us (30%)
  local copies, waits for them, and re-layouts  22.4 us (11%)
  matrix products  17.1 us (8%)
  between operations  13.5 us (7%)
  other arithmetic  9.67 us (5%)
    all_to_all x3, blocking collectives, from_everyone(): return lax.all_to_all(copies, axis, split_axis=0, concat_axis=0, tiled=True)  79.2 us
    all_gather x1, waiting for transfers between devices, shards(): lax.all_gather(group_coeffs.astype(jnp.bfloat16), 'aa', axis=0, tiled=True)  62.5 us
    scatter x1, local copies, waits for them, and re-layouts, shards(): return placed.at[ordering].set(solved.astype(jnp.bfloat16))  6.08 us
    gather x1, local copies, waits for them, and re-layouts, shards(): ordered = jnp.take(right_sides, ordering, axis=0)  5.35 us
    dot_general x1, matrix products, shards(): jnp.dot(leaf_inverse, expanded.astype(jnp.bfloat16), preferred_element_ty...  4.5 us
    scatter-add x1, other arithmetic, shards(): expanded = expanded.at[skel_rows].add(correction)  4.21 us
  transfers between devices with their start and end apart: 1, of which 1 were waited for; matrix products, arithmetic and copies ran while one was open for 0% of the time, Pallas kernels for 0%

commit v1 on v0

v1 whole, which is shorter than its diff:
```python
import functools

import jax
import jax.numpy as jnp
from jax import lax
from jax.experimental import pallas as pl
from jax.experimental.pallas import tpu as pltpu
from jax.sharding import PartitionSpec as P

MESH = pl.DeviceIdType.MESH
F32, BF16 = jnp.float32, jnp.bfloat16
LEAF, RANK, RHS = 1024, 128, 512
SIDE, NB, NZ = 4, 16, 16
PART = RHS // NB
REACH = 4


def dot(a, b):
    return jnp.dot(a, b, preferred_element_type=F32)


def wrap(value, n):
    return jnp.where(value >= n, value - n, value)


def kernel(
    sides_in, order_in, skel_in, inv_in, basis_in, core_in, trans_in, topc_in,
    out,
    sides, order, skel, inv, basis, core, trans, topc,
    point, point_t, pinv, ordered, applied, stretch,
    trans_all, coeff_all, part, part_all, topsel, top_rows, top_rows_t, core_t, zall, half, half_in, slices,
    in_sem, t_send, t_recv, x_sem, w_send, w_recv, r_send, r_recv, c_send, c_recv, z_send, z_recv, h_sem, s_send, s_recv,
):
    group, leaf = lax.axis_index("aa"), lax.axis_index("ba")
    at_z, half_id = group // 2, lax.rem(group, 2)
    at_x, at_y = leaf // SIDE, lax.rem(leaf, SIDE)
    partner = {"aa": group + 1 - 2 * half_id, "ba": leaf}
    peers = [{"aa": group, "ba": wrap(leaf + d, NB)} for d in range(1, NB)]

    def along_z(d):
        return {"aa": 2 * wrap(at_z + (d + NZ if d < 0 else d), NZ) + half_id, "ba": leaf}

    near = [d for k in range(REACH, 0, -1) for d in (k, -k)]

    loads = {}
    for i, (name, src, dst) in enumerate(
        (
            ("trans", trans_in, trans), ("order", order_in, order), ("skel", skel_in, skel), ("basis", basis_in, basis),
            ("inv", inv_in, inv), ("sides", sides_in, sides), ("topc", topc_in, topc), ("core", core_in, core),
        )
    ):
        loads[name] = pltpu.make_async_copy(src, dst, in_sem.at[i])
        loads[name].start()

    barrier = pltpu.get_barrier_semaphore()
    meet = [*peers, partner, *[along_z(d) for d in near]]
    for other in meet:
        pl.semaphore_signal(barrier, inc=1, device_id=other, device_id_type=MESH)

    def send(src, dst, send_sem, recv_sem, to):
        copy = pltpu.make_async_remote_copy(
            src_ref=src, dst_ref=dst, send_sem=send_sem, recv_sem=recv_sem, device_id=to, device_id_type=MESH
        )
        copy.start()
        return copy

    loads["trans"].wait()
    trans_all[leaf] = trans[...].astype(BF16)
    pl.semaphore_wait(barrier, len(meet))

    t_copies = [send(trans_all.at[leaf], trans_all.at[leaf], t_send.at[i], t_recv.at[i], to) for i, to in enumerate(peers)]

    loads["order"].wait()
    wanted = order[...].astype(F32)
    column = jnp.broadcast_to(wanted, (8, LEAF)).T[:, :1]
    point[...] = (column == lax.broadcasted_iota(jnp.int32, (LEAF, LEAF), 1).astype(F32)).astype(F32).astype(BF16)
    loads["skel"].wait()
    loads["basis"].wait()
    chosen = (lax.broadcasted_iota(jnp.int32, (LEAF, RANK), 0) == skel[...]).astype(F32)
    basis[...] = (basis[...].astype(F32) + chosen).astype(BF16)

    loads["topc"].wait()
    for k in range(NZ):
        topsel[:, k * RANK : (k + 1) * RANK] = topc[:, pl.ds(pl.multiple_of((2 * k + 1 - half_id) * RANK, RANK), RANK)]
        top_rows[half_id, leaf, :, k * RANK : (k + 1) * RANK] = topc[:, pl.ds(pl.multiple_of((2 * k + half_id) * RANK, RANK), RANK)]
    x_copy = send(topsel, top_rows.at[half_id, leaf], x_sem.at[0], x_sem.at[1], partner)

    loads["inv"].wait()
    reach = dot(basis[...].T, inv[...]).astype(BF16)
    gather = dot(reach, point[...]).astype(BF16)
    loads["sides"].wait()
    coeff_all[leaf] = dot(gather, sides[...]).T.astype(BF16)

    x_copy.wait_recv()
    w_copies = [
        send(top_rows.at[:, leaf], top_rows.at[:, leaf], w_send.at[i], w_recv.at[i], to) for i, to in enumerate(peers)
    ]

    loads["core"].wait()
    for copy in t_copies:
        copy.wait_recv()
    mixed = trans[...] - dot(core[...], trans_all[...].reshape(NB * RANK, RANK))
    part[...] = dot(coeff_all[leaf], mixed.astype(BF16)).astype(BF16).reshape(NB, PART, RANK)
    r_copies = []
    for i, to in enumerate(peers):
        r_copies.append(send(part.at[to["ba"]], part_all.at[leaf], r_send.at[i], r_recv.at[i], to))
    part_all[leaf] = part[leaf]

    full, quarter = RHS // 2, RHS // 4
    c_copies = {}

    def moved(along, step, place):
        x, y = place
        return (lax.rem(x + step + SIDE, SIDE), y) if along == 0 else (x, lax.rem(y + step + SIDE, SIDE))

    here = (at_x, at_y)

    def pass_on(key, place, low, count, along, step):
        block = place[0] * SIDE + place[1]
        to = moved(along, step, here)
        ref = coeff_all.at[block, pl.ds(low, count)]
        number = key[0] * 20 + key[1]
        c_copies[key] = send(ref, ref, c_send.at[number], c_recv.at[number], {"aa": group, "ba": to[0] * SIDE + to[1]})

    for h in (0, 1):
        first, second = (0, 1) if h == 0 else (1, 0)
        pass_on((h, 0), here, h * full, full, first, 1)
        pass_on((h, 1), here, h * full, full, first, -1)
        pass_on((h, 4), here, h * full, full, second, 1)
        pass_on((h, 5), here, h * full, full, second, -1)

    def c_first():
        for h in (0, 1):
            first, second = (0, 1) if h == 0 else (1, 0)
            for j, step in enumerate((-1, 1)):
                c_copies[h, j].wait_recv()
                place = moved(first, step, here)
                pass_on((h, 2 + j), place, h * full + j * quarter, quarter, first, -step)
                pass_on((h, 8 + 4 * j), place, h * full, full, second, 1)
                pass_on((h, 9 + 4 * j), place, h * full, full, second, -1)

    def c_across():
        for h in (0, 1):
            first, second = (0, 1) if h == 0 else (1, 0)
            c_copies[h, 2].wait_recv()
            c_copies[h, 3].wait_recv()
            place = moved(first, 2, here)
            pass_on((h, 16), place, h * full, full, second, 1)
            pass_on((h, 17), place, h * full, full, second, -1)

    def c_second(k, offset):
        for h in (0, 1):
            first, second = (0, 1) if h == 0 else (1, 0)
            for j, step in enumerate((-1, 1)):
                c_copies[h, 4 + 4 * k + j].wait_recv()
                place = moved(second, step, moved(first, offset, here))
                pass_on((h, 6 + 4 * k + j), place, h * full + j * quarter, quarter, second, -step)

    point_t[...] = (lax.broadcasted_iota(jnp.int32, (LEAF, LEAF), 0) == order[...]).astype(F32).astype(BF16)
    for i in range(2):
        rows = pl.ds(i * 512, 512)
        pinv[rows] = dot(point_t[rows], inv[...]).astype(BF16)

    for copy in r_copies:
        copy.wait_recv()
    total = jnp.sum(part_all[...].astype(F32), axis=0)
    zall[at_z] = total.astype(BF16)
    z_copies = {}
    for i, d in enumerate(near):
        z_copies[d] = send(zall.at[at_z], zall.at[at_z], z_send.at[i], z_recv.at[i], along_z(d))

    c_first()
    ordered[...] = dot(point[...], sides[...]).astype(BF16)
    c_across()

    relays = []
    for k in range(1, REACH + 1):
        for sign in (1, -1):
            z_copies[-sign * k].wait_recv()
            if sign < 0 and k == REACH:
                continue
            block = wrap(at_z + (sign * k if sign > 0 else NZ - k), NZ)
            n = 8 + len(relays)
            relays.append(send(zall.at[block], zall.at[block], z_send.at[n], z_recv.at[n], along_z(-sign * REACH)))

    c_second(0, 0)
    stretch_f = dot(pinv[...], basis[...])
    stretch[...] = stretch_f.astype(BF16)
    for copy in w_copies:
        copy.wait_recv()
    for k in range(2):
        top_rows_t[:, k * RANK : (k + 1) * RANK] = top_rows[k].reshape(RANK, NZ * RANK).T
    core_t[...] = core[...].T
    for copy in relays:
        copy.wait_recv()
    got = dot(jnp.concatenate([zall[k] for k in range(NZ)], axis=1), top_rows_t[...])
    half[0] = got[:, :RANK]
    half[1] = got[:, RANK:]
    h_copy = send(half.at[1 - half_id], half_in, h_sem.at[0], h_sem.at[1], partner)
    h_copy.wait_recv()
    slices[leaf] = (half[half_id] + half_in[...]).astype(BF16)
    s_copies = [send(slices.at[leaf], slices.at[leaf], s_send.at[i], s_recv.at[i], to) for i, to in enumerate(peers)]

    c_second(1, -1)
    c_second(2, 1)
    c_second(3, 2)
    for h in (0, 1):
        for k in range(4):
            c_copies[h, 6 + 4 * k].wait_recv()
            c_copies[h, 7 + 4 * k].wait_recv()
    level = dot(jnp.concatenate([coeff_all[k] for k in range(NB)], axis=1), core_t[...])
    spread = dot(stretch[...], trans[...].astype(BF16)).astype(BF16)
    lowered = level.astype(BF16).T
    for i in range(2):
        rows = pl.ds(i * 512, 512)
        applied[rows] = dot(pinv[rows], ordered[...]) - dot(stretch[rows], lowered)

    for copy in s_copies:
        copy.wait_recv()
    top = slices[...].reshape(RHS, RANK).T
    out[...] = (applied[...] - dot(spread, top)).astype(BF16)

    for copy in (*t_copies, x_copy, *w_copies, *r_copies, *c_copies.values(), *z_copies.values(), *relays, h_copy, *s_copies):
        copy.wait_send()


def shards(*args):
    dma = pltpu.SemaphoreType.DMA
    vmem = pltpu.VMEM
    scratch = [
        vmem((LEAF, RHS), BF16), vmem((1, LEAF), jnp.int32), vmem((1, RANK), jnp.int32), vmem((LEAF, LEAF), BF16),
        vmem((LEAF, RANK), BF16), vmem((RANK, NB * RANK), BF16), vmem((RANK, RANK), F32), vmem((8, 2 * NZ * RANK), BF16),
        vmem((LEAF, LEAF), BF16), vmem((LEAF, LEAF), BF16), vmem((LEAF, LEAF), BF16), vmem((LEAF, RHS), BF16),
        vmem((LEAF, RHS), F32), vmem((LEAF, RANK), BF16),
        vmem((NB, RANK, RANK), BF16), vmem((NB, RHS, RANK), BF16), vmem((NB, PART, RANK), BF16), vmem((NB, PART, RANK), BF16),
        vmem((8, NZ * RANK), BF16), vmem((2, NB, 8, NZ * RANK), BF16), vmem((NZ * RANK, 2 * RANK), BF16),
        vmem((NB * RANK, RANK), BF16), vmem((NZ, PART, RANK), BF16), vmem((2, PART, RANK), F32), vmem((PART, RANK), F32),
        vmem((NB, PART, RANK), BF16),
        dma((8,)), dma((15,)), dma((15,)), dma((2,)), dma((15,)), dma((15,)), dma((15,)), dma((15,)),
        dma((40,)), dma((40,)), dma((15,)), dma((15,)), dma((2,)), dma((15,)), dma((15,)),
    ]
    return pl.pallas_call(
        kernel,
        out_shape=jax.ShapeDtypeStruct((LEAF, RHS), BF16),
        in_specs=[pl.BlockSpec(memory_space=pl.ANY)] * 8,
        out_specs=pl.BlockSpec(memory_space=pltpu.VMEM),
        scratch_shapes=scratch,
        compiler_params=pltpu.CompilerParams(collective_id=0, has_side_effects=True, vmem_limit_bytes=67043328),
        name="woodbury",
    )(*args)


def solution(mesh):
    split = P(("aa", "ba"), None)
    return jax.shard_map(shards, mesh=mesh, in_specs=(split,) * 8, out_specs=split, check_vma=False)
```

time: 205 us -> 66.1 us (0.32)
  blocking collectives: 79.2 us -> 0 us
  Pallas kernels: 0 us -> 63.7 us
  waiting for transfers between devices: 62.5 us -> 0 us
  local copies, waits for them, and re-layouts: 22.4 us -> 2.26 us
  matrix products: 17.1 us -> 0 us
  between operations: 13.5 us -> 0.01 us
  other arithmetic: 9.67 us -> 0 us
    all_to_all x3 -> x0, blocking collectives: 79.2 us -> none  [from_everyone(): return lax.all_to_all(copies, axis, split_axis=0, concat_axis=0, tiled=True)]
    pallas_call x0 -> x1, Pallas kernels: none -> 63.7 us  [shards(): pl.pallas_call(kernel, out_shape=jax.ShapeDtypeStruct((LEAF, RHS), BF16),...]
    all_gather x1 -> x0, waiting for transfers between devices: 62.5 us -> none  [shards(): lax.all_gather(group_coeffs.astype(jnp.bfloat16), 'aa', axis=0, tiled=True)]
    dot_general x8 -> x0, matrix products: 17.1 us -> none  [the longest x1 4.5 us: shards(): jnp.dot(leaf_inverse, expanded.astype(jnp.bfloat16), preferred_element_ty...]
    gather x3 -> x0, local copies, waits for them, and re-layouts: 7.98 us -> none  [the longest x1 5.35 us: shards(): ordered = jnp.take(right_sides, ordering, axis=0)]
    scatter x1 -> x0, local copies, waits for them, and re-layouts: 6.08 us -> none  [shards(): return placed.at[ordering].set(solved.astype(jnp.bfloat16))]
    dot_general x2 -> x0, local copies, waits for them, and re-layouts: 5.87 us -> none  [the longest x1 2.93 us: shards(): jnp.dot(leaf_basis, correction.astype(jnp.bfloat16), preferred_element_ty...]
    scatter-add x1 -> x0, other arithmetic: 4.21 us -> none  [shards(): expanded = expanded.at[skel_rows].add(correction)]
  transfers between devices with their start and end apart: 1 -> 0, of which waited for: 1 -> 0; matrix products, arithmetic and copies ran while one was open for 0% -> 0% of each run, Pallas kernels for 0% -> 0%
where the time goes in v1:
time: 66.1 us; the launch traced here: 66 us
  Pallas kernels  63.7 us (96%)
  local copies, waits for them, and re-layouts  2.26 us (3%)
    pallas_call x1, Pallas kernels, shards(): pl.pallas_call(kernel, out_shape=jax.ShapeDtypeStruct((LEAF, RHS), BF16),...  63.7 us
    unnamed x1, local copies, waits for them, and re-layouts  2.26 us

profile of v1, /device:TPU:1, one launch (start us, length us, event | category | flops | bytes accessed | tf_op | source)
XLA Modules:
  0.0 66.0 jit_solution(6193011137433692813)
XLA Ops:
  0.0 63.7 %woodbury.1 = bf16[1024,512]{1,0:T(8,128)(2,1)} custom-call(bf16[1024,512]{1,0:T(8,128)(2,1)} %sides_in.1, s32[1,1024]{1,0:T(1,128)} %order_in.1, s32[1,128]{1,0:T(1,128)} %skel_in.1, bf16[1024,1024]{1,0:T(8,128)(2,1)} %inv_in.1, bf16[1024,128]{1,0:T(8,128)(2,1)} %basis_in.1, bf16[128,2048]{1,0:T(8,128)(2,1)} %core_in.1, f32[128,128]{1,0:T(8,128)} %trans_in.1, ...), custom_call_target="tpu_custom_call" | custom-call | tf_op jit(solution)/shard_map/woodbury/pallas_call | solution.py:242
  63.7 2.3 %copy.10 = bf16[1024,512]{1,0:T(8,128)(2,1)} copy(bf16[1024,512]{1,0:T(8,128)(2,1)} %woodbury.1) | data formatting | bytes 2097152

commit v2 on v1

v2 whole, which is shorter than its diff:
```python
import functools

import jax
import jax.numpy as jnp
from jax import lax
from jax.experimental import pallas as pl
from jax.experimental.pallas import tpu as pltpu
from jax.sharding import PartitionSpec as P

MESH = pl.DeviceIdType.MESH
F32, BF16 = jnp.float32, jnp.bfloat16
LEAF, RANK, RHS = 1024, 128, 512
SIDE, NB, NZ = 4, 16, 16
PART = RHS // NB


def dot(a, b):
    return jnp.dot(a, b, preferred_element_type=F32)


def wrap(value, n):
    return jnp.where(value >= n, value - n, value)


def kernel(
    sides_in, order_in, skel_in, inv_in, basis_in, core_in, trans_in, topc_in,
    out,
    sides, order, skel, inv, basis, core, trans, topc,
    point, point_t, pinv, ordered, applied, stretch,
    trans_all, coeff_all, part, part_all, topsel, top_rows, top_rows_t, core_t, zall, half, half_in, slices,
    in_sem, send_sem, t_recv, x_sem, w_recv, r_recv, c_recv, z_recv, s_recv, known_sem,
):
    group, leaf = lax.axis_index("aa"), lax.axis_index("ba")
    at_z, half_id = group // 2, lax.rem(group, 2)
    at_x, at_y = leaf // SIDE, lax.rem(leaf, SIDE)
    partner = {"aa": group + 1 - 2 * half_id, "ba": leaf}
    peers = [{"aa": group, "ba": wrap(leaf + d, NB)} for d in range(1, NB)]

    def along_z(d):
        return {"aa": 2 * wrap(at_z + (d + NZ if d < 0 else d), NZ) + half_id, "ba": leaf}

    loads = {}
    for i, (name, src, dst) in enumerate(
        (
            ("trans", trans_in, trans), ("order", order_in, order), ("skel", skel_in, skel), ("topc", topc_in, topc),
            ("basis", basis_in, basis), ("inv", inv_in, inv), ("sides", sides_in, sides), ("core", core_in, core),
        )
    ):
        loads[name] = pltpu.make_async_copy(src, dst, in_sem.at[i])
        loads[name].start()

    def signal(sem, to):
        pl.semaphore_signal(sem, inc=1, device_id=to, device_id_type=MESH)

    barrier = pltpu.get_barrier_semaphore()
    meet = [*peers, partner, along_z(1), along_z(-1)]
    for other in meet:
        signal(barrier, other)

    def send(src, dst, send_sem, recv_sem, to):
        pltpu.make_async_remote_copy(
            src_ref=src, dst_ref=dst, send_sem=send_sem, recv_sem=recv_sem, device_id=to, device_id_type=MESH
        ).start()

    def taken(ref, sem):
        pltpu.make_async_copy(ref, ref, sem).wait()

    here = (at_x, at_y)

    def moved(along, step, place):
        x, y = place
        return (lax.rem(x + step + SIDE, SIDE), y) if along == 0 else (x, lax.rem(y + step + SIDE, SIDE))

    def index(place):
        return place[0] * SIDE + place[1]

    loads["trans"].wait()
    trans_all[leaf] = trans[...].astype(BF16)
    pl.semaphore_wait(barrier, len(meet))

    for to in peers:
        send(trans_all.at[leaf], trans_all.at[leaf], send_sem.at[0], t_recv.at[0], to)
    signal(known_sem.at[0], along_z(1))
    signal(known_sem.at[0], along_z(-1))

    loads["topc"].wait()
    for k in range(NZ):
        topsel[:, k * RANK : (k + 1) * RANK] = topc[:, pl.ds(pl.multiple_of((2 * k + 1 - half_id) * RANK, RANK), RANK)]
        top_rows[half_id, leaf, :, k * RANK : (k + 1) * RANK] = topc[:, pl.ds(pl.multiple_of((2 * k + half_id) * RANK, RANK), RANK)]
    send(topsel, top_rows.at[half_id, leaf], send_sem.at[1], x_sem.at[0], partner)

    loads["order"].wait()
    wanted = order[...].astype(F32)
    column = jnp.broadcast_to(wanted, (8, LEAF)).T[:, :1]
    point[...] = (column == lax.broadcasted_iota(jnp.int32, (LEAF, LEAF), 1).astype(F32)).astype(F32).astype(BF16)
    loads["skel"].wait()
    loads["basis"].wait()
    chosen = (lax.broadcasted_iota(jnp.int32, (LEAF, RANK), 0) == skel[...]).astype(F32)
    basis[...] = (basis[...].astype(F32) + chosen).astype(BF16)

    class Gather:
        def __init__(self, piece, some, send_sem, recv_sem):
            self.piece, self.some, self.out_sem, self.in_sem = piece, some, send_sem, recv_sem

        def put(self, h, sem, place, part, along, step):
            ref = self.piece(h, index(place), part)
            send(ref, ref, self.out_sem, self.in_sem.at[sem], {"aa": group, "ba": index(moved(along, step, here))})

        def near(self):
            for h in (0, 1):
                for step in (1, -1):
                    self.put(h, 0, here, None, h, step)

        def relay_near(self):
            taken(self.some(2), self.in_sem.at[0])
            for h in (0, 1):
                for j, step in enumerate((-1, 1)):
                    self.put(h, 1, moved(h, step, here), j, h, -step)

        def over(self, k):
            if k == 3:
                taken(self.some(1), self.in_sem.at[1])
            for h in (0, 1):
                for step in (1, -1):
                    self.put(h, 2 + k, moved(h, (0, -1, 1, 2)[k], here), None, 1 - h, step)

        def relay_over(self, k):
            taken(self.some(2), self.in_sem.at[2 + k])
            for h in (0, 1):
                for j, step in enumerate((-1, 1)):
                    self.put(h, 6, moved(1 - h, step, moved(h, (0, -1, 1, 2)[k], here)), j, 1 - h, -step)

        def finish(self):
            taken(self.some(4), self.in_sem.at[6])

    full, quarter, columns = RHS // 2, RHS // 4, NZ * RANK // 2

    def coeff_piece(h, block, part):
        return coeff_all.at[block, pl.ds(h * full, full) if part is None else pl.ds(h * full + part * quarter, quarter)]

    def top_piece(h, block, part):
        return top_rows.at[h, block] if part is None else top_rows.at[h, block, :, pl.ds(part * columns, columns)]

    of_coeffs = Gather(coeff_piece, lambda n: coeff_all.at[pl.ds(0, n)], send_sem.at[2], c_recv)
    of_top = Gather(top_piece, lambda n: top_rows.at[:, pl.ds(0, n)], send_sem.at[3], w_recv)

    loads["inv"].wait()
    reach = dot(basis[...].T, inv[...]).astype(BF16)
    gather = dot(reach, point[...]).astype(BF16)
    loads["sides"].wait()
    coeff_all[leaf] = dot(gather, sides[...]).T.astype(BF16)

    taken(top_rows.at[0, 0], x_sem.at[0])
    of_top.near()
    of_top.over(0)
    of_coeffs.near()
    pl.semaphore_wait(known_sem.at[0], 2)
    signal(known_sem.at[1], along_z(2))
    signal(known_sem.at[1], along_z(-2))

    loads["core"].wait()
    taken(trans_all.at[pl.ds(0, NB - 1)], t_recv.at[0])
    mixed = trans[...] - dot(core[...], trans_all[...].reshape(NB * RANK, RANK))
    part[...] = dot(coeff_all[leaf], mixed.astype(BF16)).astype(BF16).reshape(NB, PART, RANK)
    for to in peers:
        send(part.at[to["ba"]], part_all.at[leaf], send_sem.at[4], r_recv.at[0], to)
    part_all[leaf] = part[leaf]
    pl.semaphore_wait(known_sem.at[1], 2)
    signal(known_sem.at[2], along_z(4))
    signal(known_sem.at[2], along_z(-4))
    of_top.relay_near()
    of_top.over(1)
    of_top.over(2)

    point_t[...] = (lax.broadcasted_iota(jnp.int32, (LEAF, LEAF), 0) == order[...]).astype(F32).astype(BF16)
    for i in range(2):
        rows = pl.ds(i * 512, 512)
        pinv[rows] = dot(point_t[rows], inv[...]).astype(BF16)
    of_top.over(3)
    for k in range(3):
        of_top.relay_over(k)
    of_coeffs.relay_near()
    core_t[...] = core[...].T
    pl.semaphore_wait(known_sem.at[2], 2)

    taken(part_all.at[pl.ds(0, NB - 1)], r_recv.at[0])
    total = jnp.sum(part_all[...].astype(F32), axis=0)
    zall[at_z] = total.astype(BF16)
    for d in (NZ // 2, *[d for k in range(NZ // 2 - 1, 0, -1) for d in (k, -k)]):
        send(zall.at[at_z], zall.at[at_z], send_sem.at[5], z_recv.at[0], along_z(d))

    for k in range(3):
        of_coeffs.over(k)
    ordered[...] = dot(point[...], sides[...]).astype(BF16)
    of_top.relay_over(3)
    stretch[...] = dot(pinv[...], basis[...]).astype(BF16)
    of_coeffs.over(3)

    for i in range(2):
        rows = pl.ds(i * 512, 512)
        applied[rows] = dot(pinv[rows], ordered[...])
    spread = dot(stretch[...], trans[...].astype(BF16)).astype(BF16)
    of_top.finish()
    for k in range(2):
        top_rows_t[:, k * RANK : (k + 1) * RANK] = top_rows[k].reshape(RANK, NZ * RANK).T
    for k in range(3):
        of_coeffs.relay_over(k)
    taken(zall.at[pl.ds(0, NZ - 1)], z_recv.at[0])
    got = dot(jnp.concatenate([zall[k] for k in range(NZ)], axis=1), top_rows_t[...])
    half[0] = got[:, :RANK]
    half[1] = got[:, RANK:]
    send(half.at[1 - half_id], half_in, send_sem.at[6], x_sem.at[1], partner)
    of_coeffs.relay_over(3)
    taken(half_in, x_sem.at[1])
    slices[leaf] = (half[half_id] + half_in[...]).astype(BF16)
    for to in peers:
        send(slices.at[leaf], slices.at[leaf], send_sem.at[7], s_recv.at[0], to)

    of_coeffs.finish()
    lowered = dot(jnp.concatenate([coeff_all[k] for k in range(NB)], axis=1), core_t[...]).astype(BF16).T
    applied[...] -= dot(stretch[...], lowered)
    for i, ref in enumerate(
        (
            trans_all.at[pl.ds(0, NB - 1)], topsel, coeff_all.at[pl.ds(0, NB - 1)], top_rows.at[:, pl.ds(0, NB - 1)],
            part_all.at[pl.ds(0, NB - 1)], zall.at[pl.ds(0, NZ - 1)], half_in,
        )
    ):
        taken(ref, send_sem.at[i])

    taken(slices.at[pl.ds(0, NB - 1)], s_recv.at[0])
    top = slices[...].reshape(RHS, RANK).T
    out[...] = (applied[...] - dot(spread, top)).astype(BF16)
    taken(slices.at[pl.ds(0, NB - 1)], send_sem.at[7])


def shards(*args):
    dma = pltpu.SemaphoreType.DMA
    vmem = pltpu.VMEM
    scratch = [
        vmem((LEAF, RHS), BF16), vmem((1, LEAF), jnp.int32), vmem((1, RANK), jnp.int32), vmem((LEAF, LEAF), BF16),
        vmem((LEAF, RANK), BF16), vmem((RANK, NB * RANK), BF16), vmem((RANK, RANK), F32), vmem((8, 2 * NZ * RANK), BF16),
        vmem((LEAF, LEAF), BF16), vmem((LEAF, LEAF), BF16), vmem((LEAF, LEAF), BF16), vmem((LEAF, RHS), BF16),
        vmem((LEAF, RHS), F32), vmem((LEAF, RANK), BF16),
        vmem((NB, RANK, RANK), BF16), vmem((NB, RHS, RANK), BF16), vmem((NB, PART, RANK), BF16), vmem((NB, PART, RANK), BF16),
        vmem((8, NZ * RANK), BF16), vmem((2, NB, 8, NZ * RANK), BF16), vmem((NZ * RANK, 2 * RANK), BF16),
        vmem((NB * RANK, RANK), BF16), vmem((NZ, PART, RANK), BF16), vmem((2, PART, RANK), F32), vmem((PART, RANK), F32),
        vmem((NB, PART, RANK), BF16),
        dma((8,)), dma((8,)), dma((1,)), dma((2,)), dma((7,)), dma((1,)), dma((7,)), dma((1,)), dma((1,)),
        pltpu.SemaphoreType.REGULAR((3,)),
    ]
    return pl.pallas_call(
        kernel,
        out_shape=jax.ShapeDtypeStruct((LEAF, RHS), BF16),
        in_specs=[pl.BlockSpec(memory_space=pl.ANY)] * 8,
        out_specs=pl.BlockSpec(memory_space=pltpu.VMEM),
        scratch_shapes=scratch,
        compiler_params=pltpu.CompilerParams(collective_id=0, has_side_effects=True, vmem_limit_bytes=40 * 2**20),
        name="woodbury",
    )(*[pltpu.with_memory_space_constraint(a, pltpu.HBM) for a in args])


def solution(mesh):
    split = P(("aa", "ba"), None)
    return jax.shard_map(shards, mesh=mesh, in_specs=(split,) * 8, out_specs=split, check_vma=False)
```

time: 66.1 us -> 47.6 us (0.72)
  Pallas kernels: 63.7 us -> 46.5 us
  local copies, waits for them, and re-layouts: 2.26 us -> 0.97 us
    pallas_call x1, Pallas kernels: 63.7 us -> 46.5 us  [shards(): pl.pallas_call(kernel, out_shape=jax.ShapeDtypeStruct((LEAF, RHS), BF16),...]
    unnamed x1, local copies, waits for them, and re-layouts: 2.26 us -> 0.97 us
where the time goes in v2:
time: 47.6 us; the launch traced here: 47.5 us
  Pallas kernels  46.5 us (98%)
  local copies, waits for them, and re-layouts  0.97 us (2%)
    pallas_call x1, Pallas kernels, shards(): pl.pallas_call(kernel, out_shape=jax.ShapeDtypeStruct((LEAF, RHS), BF16),...  46.5 us
    unnamed x1, local copies, waits for them, and re-layouts  0.97 us

profile of v2, /device:TPU:1, one launch (start us, length us, event | category | flops | bytes accessed | tf_op | source)
XLA Modules:
  0.0 47.5 jit_solution(7384466696168747855)
XLA Ops:
  0.0 46.5 %woodbury.1 = bf16[1024,512]{1,0:T(8,128)(2,1)S(1)} custom-call(bf16[1024,512]{1,0:T(8,128)(2,1)} %sides_in.1, s32[1,1024]{1,0:T(1,128)} %order_in.1, s32[1,128]{1,0:T(1,128)} %skel_in.1, bf16[1024,1024]{1,0:T(8,128)(2,1)} %inv_in.1, bf16[1024,128]{1,0:T(8,128)(2,1)} %basis_in.1, bf16[128,2048]{1,0:T(8,128)(2,1)} %core_in.1, f32[128,128]{1,0:T(8,128)} %trans_in.1, ...), custom_call_target="tpu_custom_call" | custom-call | tf_op jit(solution)/shard_map/woodbury/pallas_call | solution.py:251
  46.5 1.0 %copy.10 = bf16[1024,512]{1,0:T(8,128)(2,1)} copy(bf16[1024,512]{1,0:T(8,128)(2,1)S(1)} %woodbury.1) | data formatting | bytes 2097152

commit v3 on v2

--- a/solution.py
+++ b/solution.py
@@ -34,7 +34,11 @@
     at_z, half_id = group // 2, lax.rem(group, 2)
     at_x, at_y = leaf // SIDE, lax.rem(leaf, SIDE)
     partner = {"aa": group + 1 - 2 * half_id, "ba": leaf}
-    peers = [{"aa": group, "ba": wrap(leaf + d, NB)} for d in range(1, NB)]
+    def index(place):
+        return place[0] * SIDE + place[1]
+
+    far = [(2, 2), (2, 1), (2, 3), (1, 2), (3, 2), (2, 0), (0, 2), (1, 1), (3, 3), (1, 3), (3, 1), (1, 0), (3, 0), (0, 1), (0, 3)]
+    peers = [{"aa": group, "ba": index((wrap(at_x + dx, SIDE), wrap(at_y + dy, SIDE)))} for dx, dy in far]
 
     def along_z(d):
         return {"aa": 2 * wrap(at_z + (d + NZ if d < 0 else d), NZ) + half_id, "ba": leaf}
@@ -71,9 +75,6 @@
         x, y = place
         return (lax.rem(x + step + SIDE, SIDE), y) if along == 0 else (x, lax.rem(y + step + SIDE, SIDE))
 
-    def index(place):
-        return place[0] * SIDE + place[1]
-
     loads["trans"].wait()
     trans_all[leaf] = trans[...].astype(BF16)
     pl.semaphore_wait(barrier, len(meet))
@@ -152,7 +153,6 @@
 
     taken(top_rows.at[0, 0], x_sem.at[0])
     of_top.near()
-    of_top.over(0)
     of_coeffs.near()
     pl.semaphore_wait(known_sem.at[0], 2)
     signal(known_sem.at[1], along_z(2))
@@ -168,6 +168,7 @@
     pl.semaphore_wait(known_sem.at[1], 2)
     signal(known_sem.at[2], along_z(4))
     signal(known_sem.at[2], along_z(-4))
+    of_top.over(0)
     of_top.relay_near()
     of_top.over(1)
     of_top.over(2)
@@ -176,9 +177,6 @@
     for i in range(2):
         rows = pl.ds(i * 512, 512)
         pinv[rows] = dot(point_t[rows], inv[...]).astype(BF16)
-    of_top.over(3)
-    for k in range(3):
-        of_top.relay_over(k)
     of_coeffs.relay_near()
     core_t[...] = core[...].T
     pl.semaphore_wait(known_sem.at[2], 2)
@@ -189,6 +187,9 @@
     for d in (NZ // 2, *[d for k in range(NZ // 2 - 1, 0, -1) for d in (k, -k)]):
         send(zall.at[at_z], zall.at[at_z], send_sem.at[5], z_recv.at[0], along_z(d))
 
+    of_top.over(3)
+    for k in range(3):
+        of_top.relay_over(k)
     for k in range(3):
         of_coeffs.over(k)
     ordered[...] = dot(point[...], sides[...]).astype(BF16)
@@ -216,8 +217,14 @@
     for to in peers:
         send(slices.at[leaf], slices.at[leaf], send_sem.at[7], s_recv.at[0], to)
 
+    def of_blocks(h, steps):
+        blocks = [index(moved(1 - h, step, moved(h, other, here))) for step in steps for other in range(SIDE)]
+        left = jnp.concatenate([coeff_all[k, h * full : (h + 1) * full] for k in blocks], axis=1)
+        return dot(left, jnp.concatenate([core_t[pl.ds(pl.multiple_of(k * RANK, RANK), RANK)] for k in blocks], axis=0))
+
+    early = [of_blocks(h, (0, 1, -1)) for h in (0, 1)]
     of_coeffs.finish()
-    lowered = dot(jnp.concatenate([coeff_all[k] for k in range(NB)], axis=1), core_t[...]).astype(BF16).T
+    lowered = jnp.concatenate([early[h] + of_blocks(h, (2,)) for h in (0, 1)], axis=0).astype(BF16).T
     applied[...] -= dot(stretch[...], lowered)
     for i, ref in enumerate(
         (

time: 47.6 us -> 44.4 us (0.933)
  Pallas kernels: 46.5 us -> 43.3 us
    pallas_call x1, Pallas kernels: 46.5 us -> 43.3 us  [shards(): pl.pallas_call(kernel, out_shape=jax.ShapeDtypeStruct((LEAF, RHS), BF16),...]
where the time goes in v3:
time: 44.4 us; the launch traced here: 44.3 us
  Pallas kernels  43.3 us (98%)
  local copies, waits for them, and re-layouts  0.97 us (2%)
    pallas_call x1, Pallas kernels, shards(): pl.pallas_call(kernel, out_shape=jax.ShapeDtypeStruct((LEAF, RHS), BF16),...  43.3 us
    unnamed x1, local copies, waits for them, and re-layouts  0.97 us

profile of v3, /device:TPU:1, one launch (start us, length us, event | category | flops | bytes accessed | tf_op | source)
XLA Modules:
  0.0 44.3 jit_solution(17230296594523521146)
XLA Ops:
  0.0 43.3 %woodbury.1 = bf16[1024,512]{1,0:T(8,128)(2,1)S(1)} custom-call(bf16[1024,512]{1,0:T(8,128)(2,1)} %sides_in.1, s32[1,1024]{1,0:T(1,128)} %order_in.1, s32[1,128]{1,0:T(1,128)} %skel_in.1, bf16[1024,1024]{1,0:T(8,128)(2,1)} %inv_in.1, bf16[1024,128]{1,0:T(8,128)(2,1)} %basis_in.1, bf16[128,2048]{1,0:T(8,128)(2,1)} %core_in.1, f32[128,128]{1,0:T(8,128)} %trans_in.1, ...), custom_call_target="tpu_custom_call" | custom-call | tf_op jit(solution)/shard_map/woodbury/pallas_call | solution.py:258
  43.3 1.0 %copy.10 = bf16[1024,512]{1,0:T(8,128)(2,1)} copy(bf16[1024,512]{1,0:T(8,128)(2,1)S(1)} %woodbury.1) | data formatting | bytes 2097152

commit v4 on v3

--- a/solution.py
+++ b/solution.py
@@ -189,9 +189,9 @@
 
     of_top.over(3)
     for k in range(3):
+        of_coeffs.over(k)
+    for k in range(3):
         of_top.relay_over(k)
-    for k in range(3):
-        of_coeffs.over(k)
     ordered[...] = dot(point[...], sides[...]).astype(BF16)
     of_top.relay_over(3)
     stretch[...] = dot(pinv[...], basis[...]).astype(BF16)
@@ -201,11 +201,11 @@
         rows = pl.ds(i * 512, 512)
         applied[rows] = dot(pinv[rows], ordered[...])
     spread = dot(stretch[...], trans[...].astype(BF16)).astype(BF16)
+    for k in range(3):
+        of_coeffs.relay_over(k)
     of_top.finish()
     for k in range(2):
         top_rows_t[:, k * RANK : (k + 1) * RANK] = top_rows[k].reshape(RANK, NZ * RANK).T
-    for k in range(3):
-        of_coeffs.relay_over(k)
     taken(zall.at[pl.ds(0, NZ - 1)], z_recv.at[0])
     got = dot(jnp.concatenate([zall[k] for k in range(NZ)], axis=1), top_rows_t[...])
     half[0] = got[:, :RANK]
@@ -225,7 +225,6 @@
     early = [of_blocks(h, (0, 1, -1)) for h in (0, 1)]
     of_coeffs.finish()
     lowered = jnp.concatenate([early[h] + of_blocks(h, (2,)) for h in (0, 1)], axis=0).astype(BF16).T
-    applied[...] -= dot(stretch[...], lowered)
     for i, ref in enumerate(
         (
             trans_all.at[pl.ds(0, NB - 1)], topsel, coeff_all.at[pl.ds(0, NB - 1)], top_rows.at[:, pl.ds(0, NB - 1)],
@@ -236,7 +235,8 @@
 
     taken(slices.at[pl.ds(0, NB - 1)], s_recv.at[0])
     top = slices[...].reshape(RHS, RANK).T
-    out[...] = (applied[...] - dot(spread, top)).astype(BF16)
+    both = dot(jnp.concatenate([stretch[...], spread], axis=1), jnp.concatenate([lowered, top], axis=0))
+    out[...] = (applied[...] - both).astype(BF16)
     taken(slices.at[pl.ds(0, NB - 1)], send_sem.at[7])
 
 

time: 44.4 us -> 44.4 us (level)
  no operation moved by 1% of the time
where the time goes in v4:
time: 44.4 us; the launch traced here: 44.3 us
  Pallas kernels  43.4 us (98%)
  local copies, waits for them, and re-layouts  0.97 us (2%)
    pallas_call x1, Pallas kernels, shards(): pl.pallas_call(kernel, out_shape=jax.ShapeDtypeStruct((LEAF, RHS), BF16),...  43.4 us
    unnamed x1, local copies, waits for them, and re-layouts  0.97 us

profile of v4, /device:TPU:1, one launch (start us, length us, event | category | flops | bytes accessed | tf_op | source)
XLA Modules:
  0.0 44.3 jit_solution(11931797090584955748)
XLA Ops:
  0.0 43.4 %woodbury.1 = bf16[1024,512]{1,0:T(8,128)(2,1)S(1)} custom-call(bf16[1024,512]{1,0:T(8,128)(2,1)} %sides_in.1, s32[1,1024]{1,0:T(1,128)} %order_in.1, s32[1,128]{1,0:T(1,128)} %skel_in.1, bf16[1024,1024]{1,0:T(8,128)(2,1)} %inv_in.1, bf16[1024,128]{1,0:T(8,128)(2,1)} %basis_in.1, bf16[128,2048]{1,0:T(8,128)(2,1)} %core_in.1, f32[128,128]{1,0:T(8,128)} %trans_in.1, ...), custom_call_target="tpu_custom_call" | custom-call | tf_op jit(solution)/shard_map/woodbury/pallas_call | solution.py:258
  43.4 1.0 %copy.10 = bf16[1024,512]{1,0:T(8,128)(2,1)} copy(bf16[1024,512]{1,0:T(8,128)(2,1)S(1)} %woodbury.1) | data formatting | bytes 2097152
